TPU v7x, 256 devices: a whole 4x4x8 slice. The times are simulated.
256 devices in a mesh: expert: 8 (over x, core), latent: 32 (over y, z).
Axes of the slice: x: 4, y: 4, z: 8, core: 2. Of those that a mesh axis runs over, the one named last changes fastest.
Arguments:
- tokens: bfloat16 [2048, 2560], P(('expert', 'latent')), may hold values from -6 to 6
- route: int32 [2048, 1], P(('expert', 'latent')), may hold values from 0 to 7; in each aligned block of 8 rows (0 to 7, 8 to 15, ...) at most 2 rows name the same one
- blocks: int32 [2048, 64], P(('expert', 'latent')), may hold values from 0 to 255, all different within a row
- weight: bfloat16 [8, 2560, 32768], P('expert', None, 'latent'), may hold values from -0.125 to 0.125
- enc_bias: float32 [8, 32768], P('expert', 'latent'), may hold values from -3 to 3
- dec_bias: float32 [2560], replicated, may hold values from -3 to 3
Outputs:
- grad_weight: bfloat16 [8, 2560, 32768], P('expert', None, 'latent')
- grad_enc: float32 [8, 32768], P('expert', 'latent')
- grad_dec: float32 [2560], replicated
- loss: float32 [], replicated
Inputs may be any that keep to these rules, and one draw needn't show every extreme that they name: `route`: within the rows of one device (aligned blocks of 8 rows) no expert is named by more than 2 rows. Each row lists 64 different blocks.
All inputs are finite; a program needn't handle non-finite values.
Results may differ from a plain program's by a relative error of at most 0.012.
The roundings to bfloat16 on the way count: a program that leaves them out, or rounds other values in their place, can miss the bound.
Values may be sent and summed in bfloat16 or wider, within the bound.
No kernel may reach another device: no remote copies, remote signals or barrier semaphores. Data moves between devices by JAX's collectives and lax.ppermute only.
A program may use at most 128 MiB of HBM per device.

v0:
```python
import jax
import jax.numpy as jnp
from jax import lax
from jax.sharding import PartitionSpec as P

BLK = 128
CAP = 2


def shards(tokens, route, blocks, weight, enc_bias, dec_bias):
    n_expert = lax.axis_size("expert")
    n_latent = lax.axis_size("latent")
    width = tokens.shape[1]
    list_len = blocks.shape[1]
    expert_of = route[:, 0]
    one_hot = (expert_of[:, None] == jnp.arange(n_expert, dtype=jnp.int32)[None, :]).astype(
        jnp.int32
    )
    earlier = jnp.sum((jnp.cumsum(one_hot, axis=0) - one_hot) * one_hot, axis=1)
    target = expert_of * CAP + earlier
    send_rows = jnp.zeros((n_expert * CAP, width), jnp.bfloat16).at[target].set(tokens)
    send_rows = send_rows.reshape(n_expert, CAP, width)
    send_lists = jnp.full((n_expert * CAP, list_len), -1, jnp.int32).at[target].set(blocks)
    send_lists = send_lists.reshape(n_expert, CAP, list_len)
    got_rows, got_lists = (
        lax.all_to_all(send_rows, "expert", split_axis=0, concat_axis=0, tiled=True),
        lax.all_to_all(send_lists, "expert", split_axis=0, concat_axis=0, tiled=True),
    )
    all_rows, all_lists = (
        lax.all_gather(got_rows[None], "latent", axis=0, tiled=True),
        lax.all_gather(got_lists[None], "latent", axis=0, tiled=True),
    )
    token_rows = all_rows.reshape(-1, width)
    listed = all_lists.reshape(-1, list_len)
    row_count = token_rows.shape[0]
    valid = (listed[:, 0] >= 0).astype(jnp.float32)
    slice_index = lax.axis_index("latent")
    weights_here = weight[0]
    per_slice = weights_here.shape[1] // BLK
    own_blocks = slice_index * per_slice + jnp.arange(per_slice, dtype=jnp.int32)
    chosen = jnp.any(listed[:, :, None] == own_blocks[None, None, :], axis=1).astype(jnp.float32)
    mask = jnp.repeat(chosen, BLK, axis=1)
    rows_f32 = token_rows.astype(jnp.float32)
    shifted = (rows_f32 - dec_bias).astype(jnp.bfloat16)
    pre_act = jnp.dot(shifted, weights_here, preferred_element_type=jnp.float32) + enc_bias[0]
    active = jnp.maximum(pre_act, 0.0) * mask
    active_bf = active.astype(jnp.bfloat16)
    share = row_count // n_latent
    first_row = slice_index * share
    along_width = (((1,), (1,)), ((), ()))
    partial_sum = lax.dot_general(
        active_bf, weights_here, along_width, preferred_element_type=jnp.float32
    )
    summed = lax.psum(partial_sum, "latent")
    error_all = (summed + dec_bias - rows_f32) * valid[:, None]
    error_bf = error_all.astype(jnp.bfloat16)
    error_share = lax.dynamic_slice_in_dim(error_all, first_row, share, 0)
    grad_act = jnp.dot(error_bf, weights_here, preferred_element_type=jnp.float32)
    grad_pre = grad_act * (pre_act > 0.0).astype(jnp.float32) * mask
    grad_pre_bf = grad_pre.astype(jnp.bfloat16)
    along_rows = (((0,), (0,)), ((), ()))
    grad_here = lax.dot_general(
        shifted, grad_pre_bf, along_rows, preferred_element_type=jnp.float32
    )
    grad_here = grad_here + lax.dot_general(
        error_bf, active_bf, along_rows, preferred_element_type=jnp.float32
    )
    grad_bias = jnp.sum(grad_pre, axis=0)
    pulled = jnp.dot(
        weights_here, grad_bias.astype(jnp.bfloat16), preferred_element_type=jnp.float32
    )
    bias_term = jnp.sum(error_share, axis=0) - pulled
    loss_term = 0.5 * jnp.sum(error_share * error_share)
    grad_dec, loss_sum = lax.psum((bias_term, loss_term), ("expert", "latent"))
    loss = loss_sum / (tokens.shape[0] * n_expert * n_latent)
    return (grad_here.astype(jnp.bfloat16)[None], grad_bias[None], grad_dec, loss)


def solution(mesh):
    return jax.shard_map(
        shards,
        mesh=mesh,
        in_specs=(
            P(("expert", "latent"), None),
            P(("expert", "latent"), None),
            P(("expert", "latent"), None),
            P("expert", None, "latent"),
            P("expert", "latent"),
            P(),
        ),
        out_specs=(P("expert", None, "latent"), P("expert", "latent"), P(), P()),
        check_vma=False,
    )
```

profile of v0, /device:TPU:1, one launch (start us, length us, event | category | flops | bytes accessed | tf_op | source)
XLA Modules:
  0.0 402.3 jit_solution(3232776257881222928)
XLA Ops:
  7.2 0.0 copy-start.4
  7.2 0.0 all-gather.4.cloned.1.call-start
  7.2 0.7 fusion.24
  8.0 0.8 select_reduce_fusion
  8.8 0.7 fusion.25
  9.5 0.9 scatter_custom_fusion
  10.4 11.2 %all_to_all.10 = bf16[8,2,2560]{2,1,0:T(2,128)(2,1)} all-to-all(bf16[8,2,2560]{2,1,0:T(2,128)(2,1)S(1)} %reshape.33), channel_id=1, replica_groups=mesh['expert'=8,'latent'=32] {'expert'}, dimensions={0} | all-to-all | bytes 163840 | tf_op jit(solution)/shard_map/all_to_all | solution.py:26
  21.6 0.0 all-gather.4.cloned.1.call-update
  21.7 0.8 scatter_custom_fusion.1
  22.4 0.7 reshape.68
  23.1 4.0 all-to-all-start.1
  27.1 0.0 all-reduce.3.cloned.1.call-start
  27.1 4.5 %all-to-all-done.1 = s32[8,1,128]{2,1,0:T(1,128)S(1)} async-done(((s32[8,1,128]{2,1,0:T(1,128)}), s32[8,1,128]{2,1,0:T(1,128)S(1)}, u32[]{:S(2)}, u32[]{:S(2)}) %all-to-all-start.1) | async-done | bytes 4128 | tf_op jit(solution)/shard_map/all_to_all | solution.py:27
  31.6 0.5 broadcast.43
  32.2 0.7 reduce.4
  32.8 0.1 reshape.69
  32.9 40.8 %all-gather.1 = s32[256,2,64]{2,1,0:T(2,128)S(1)} all-gather(s32[8,2,64]{2,1,0:T(2,128)S(1)} %reshape.69), channel_id=3, replica_groups=mesh['expert'=8,'latent'=32] {'latent'}, dimensions={0}, use_global_device_ids=true | all-gather | bytes 135168 | tf_op jit(solution)/shard_map/all_gather | solution.py:31
  73.7 0.1 copy.12
  73.8 0.2 compare_reduce_fusion
  74.1 0.1 copy.13
  74.2 24.0 %all-gather.4.cloned.1.call-done = bf16[256,2,2560]{2,1,0:T(2,128)(2,1)} async-done(((bf16[8,2,2560]{2,1,0:T(2,128)(2,1)}), bf16[256,2,2560]{2,1,0:T(2,128)(2,1)}) %all-gather.4.cloned.1.call-update) | async-done | bytes 2621456 | tf_op jit(solution)/shard_map/all_gather | solution.py:30
  98.1 3.5 convert_element_type.56
  101.7 0.0 copy-done.4
  101.7 2.3 subtract_convert_fusion
  104.0 0.0 copy-start.6
  104.0 2.6 convert_element_type.47
  106.6 0.0 slice-start.2
  106.6 0.6 broadcast_in_dim.32
  107.2 0.0 copy-start.1
  107.2 0.0 copy-done.6
  107.2 0.0 slice-start.3
  107.3 8.7 %fusion.11 = (bf16[512,1024]{1,0:T(8,128)(2,1)S(1)}, f32[512,1024]{1,0:T(8,128)}) fusion(f32[64,8,8,128]{3,2,1,0:T(8,128)S(1)} %bitcast.51, f32[1024]{0:T(1024)S(1)} %bitcast.57, bf16[512,2560]{1,0:T(8,128)(2,1)} %convert_element_type.47, bf16[1,2560,1024]{2,1,0:T(8,128)(2,1)} %param.9), kind=kOutput, calls=%fused_computation.19 | convolution fusion | flops 2686451712 | bytes 13111296 | tf_op jit(solution)/shard_map/dot_general | solution.py:45
  116.0 0.0 copy-done.1
  116.0 0.0 copy-start.3
  116.0 1.0 copy-done.3
  117.0 0.0 slice-done.2
  117.0 0.0 slice-done.3
  117.0 4.7 %fusion.4 = f32[512,2560]{1,0:T(8,128)} fusion(bf16[512,1024]{1,0:T(8,128)(2,1)S(1)} %get-tuple-element.8, bf16[1,2560,1024]{2,1,0:T(8,128)(2,1)S(1)} %bitcast.46), kind=kOutput, calls=%fused_computation.7 | convolution fusion | flops 2684354560 | bytes 11534336 | tf_op jit(solution)/shard_map/dot_general | solution.py:51
  121.7 0.0 copy-start
  121.7 0.0 all-reduce.3.cloned.1.call-update
  121.7 0.1 convert_reduce_fusion
  121.8 1.6 copy-done
  123.4 2.9 reshape.36
  126.3 0.0 copy-start.2
  126.4 168.2 %all-reduce.3.cloned.1.call-done = f32[512,2560]{1,0:T(8,128)} async-done(((f32[512,2560]{1,0:T(8,128)}), f32[512,2560]{1,0:T(8,128)}) %all-reduce.3.cloned.1.call-update) | async-done | bytes 5242896 | tf_op jit(solution)/shard_map/psum | solution.py:54
  294.5 0.0 copy-start.7
  294.5 4.9 %subtract_multiply_fusion = f32[512,2560]{1,0:T(8,128)S(1)} fusion(f32[512,2560]{1,0:T(8,128)} %reshape.36, f32[512,2560]{1,0:T(8,128)} %all-reduce.3.cloned.1.call-done, f32[512]{0:T(512)S(1)} %convert_reduce_fusion, f32[2560]{0:T(1024)S(1)} %copy-done.4), kind=kLoop, calls=%fused_computation.11 | loop fusion | flops 3932160 | bytes 15740928 | tf_op jit(solution)/shard_map/mul | solution.py:55
  299.4 0.0 copy-done.2
  299.5 0.0 copy-done.7
  299.5 0.0 slice-start.1
  299.5 5.9 %fusion.26 = (f32[1024]{0:T(1024)S(1)}, bf16[512,1024]{1,0:T(8,128)(2,1)S(1)}) fusion(f32[64,8,8,128]{3,2,1,0:T(8,128)S(1)} %bitcast.52, bf16[1,2560,1024]{2,1,0:T(8,128)(2,1)} %param.9, f32[512,2560]{1,0:T(8,128)S(1)} %subtract_multiply_fusion, f32[512,1024]{1,0:T(8,128)S(1)} %copy-done.7, f32[1024]{0:T(1024)S(1)} %bitcast.58), kind=kOutput, calls=%fused_computation.40 | convolution fusion | flops 2688809984 | bytes 15736832 | tf_op jit(solution)/shard_map/dot_general | solution.py:58
  305.4 0.0 copy-start.5
  305.4 0.0 slice-done
  305.4 0.0 slice-done.1
  305.4 0.0 slice-start.4
  305.5 3.0 fusion.9
  308.5 0.0 slice-start.5
  308.5 6.5 %fusion.8 = bf16[1,2560,1024]{2,1,0:T(8,128)(2,1)} fusion(f32[2560,1024]{1,0:T(8,128)S(1)} %fusion.9, bf16[512,1024]{1,0:T(8,128)(2,1)} %copy-done.3, f32[512,2560]{1,0:T(8,128)S(1)} %subtract_multiply_fusion), kind=kOutput, calls=%fused_computation.14 | convolution fusion | flops 2690908160 | bytes 22020096 | tf_op jit(solution)/shard_map/dot_general | solution.py:65
  315.0 0.6 multiply_reduce_fusion
  315.6 0.0 copy-done.5
  315.6 0.0 slice-done.4
  315.6 0.0 slice-done.5
  315.6 1.5 fusion.16
  317.8 75.9 %all-reduce = (f32[2560]{0:T(1024)}, f32[]{:T(128)}) all-reduce(f32[2560]{0:T(1024)S(1)} %sub.28, f32[]{:T(128)S(6)} %mul_shard_map.3), channel_id=1, replica_groups=mesh['expert'=8,'latent'=32] {'expert','latent'}, use_global_device_ids=true, to_apply=%region_8.9 | all-reduce | flops 2561 | bytes 20488 | tf_op jit(solution)/shard_map/psum | solution.py:74
  (11 shorter events, 0.1 us)
Async XLA Ops:
  7.2 94.5 %copy-start.4 = (f32[2560]{0:T(1024)S(1)}, f32[2560]{0:T(1024)}, u32[]{:S(2)}) copy-start(f32[2560]{0:T(1024)} %param.11) | copy-start | bytes 30724
  7.2 91.0 %all-gather.4.cloned.1.call-start = ((), (), s32[]{:S(2)}) async-start(), calls=%async_computation.3 | async-start | bytes 2703360 | tf_op jit(solution)/shard_map/all_gather | solution.py:30
  23.1 8.5 %all-to-all-start.1 = ((s32[8,1,128]{2,1,0:T(1,128)}), s32[8,1,128]{2,1,0:T(1,128)S(1)}, u32[]{:S(2)}, u32[]{:S(2)}) async-start(s32[8,1,128]{2,1,0:T(1,128)} %reshape.68), calls=%async_computation.1 | async-start | bytes 8192 | tf_op jit(solution)/shard_map/all_to_all | solution.py:27
  27.1 267.4 %all-reduce.3.cloned.1.call-start = ((), (), s32[]{:S(2)}) async-start(), calls=%async_computation.2 | async-start | bytes 10485760 | tf_op jit(solution)/shard_map/psum | solution.py:54
  104.0 3.2 copy-start.6
  106.6 10.4 %slice-start.2 = ((s8[5242880]{0:T(1024)(128)(4,1)}), s8[4194304]{0:T(1024)(128)(4,1)S(1)}, s32[]{:S(2)}) async-start(s8[5242880]{0:T(1024)(128)(4,1)} %bitcast.45), calls=%async_computation.6 | async-start | bytes 8388608
  107.2 8.8 %copy-start.1 = (f32[512,8,128]{2,1,0:T(8,128)}, f32[512,8,128]{2,1,0:T(8,128)S(1)}, u32[]{:S(2)}) copy-start(f32[512,8,128]{2,1,0:T(8,128)S(1)} %broadcast_in_dim.32) | copy-start | bytes 6291460
  107.2 9.7 %slice-start.3 = ((s8[5242880]{0:T(1024)(128)(4,1)}), s8[1048576]{0:T(1024)(128)(4,1)S(1)}, s32[]{:S(2)}) async-start(s8[5242880]{0:T(1024)(128)(4,1)} %bitcast.45), calls=%async_computation.7 | async-start | bytes 2097152
  116.0 1.0 copy-start.3
  121.7 1.7 copy-start
  126.3 173.1 %copy-start.2 = (f32[512,8,128]{2,1,0:T(8,128)S(1)}, f32[512,8,128]{2,1,0:T(8,128)}, u32[]{:S(2)}) copy-start(f32[512,8,128]{2,1,0:T(8,128)} %copy-done.1) | copy-start | bytes 6291460
  294.5 4.9 %copy-start.7 = (f32[512,1024]{1,0:T(8,128)S(1)}, f32[512,1024]{1,0:T(8,128)}, u32[]{:S(2)}) copy-start(f32[512,1024]{1,0:T(8,128)} %get-tuple-element.9) | copy-start | bytes 6291460
  294.5 10.9 %slice-start = ((s8[5242880]{0:T(1024)(128)(4,1)}), s8[1048576]{0:T(1024)(128)(4,1)S(1)}, s32[]{:S(2)}) async-start(s8[5242880]{0:T(1024)(128)(4,1)} %bitcast.42), calls=%async_computation.4 | async-start | bytes 2097152
  299.5 6.0 %slice-start.1 = ((s8[5242880]{0:T(1024)(128)(4,1)}), s8[4194304]{0:T(1024)(128)(4,1)S(1)}, s32[]{:S(2)}) async-start(s8[5242880]{0:T(1024)(128)(4,1)} %bitcast.42), calls=%async_computation.5 | async-start | bytes 8388608
  305.4 10.2 %copy-start.5 = (f32[1024]{0:T(1024)}, f32[1024]{0:T(1024)S(1)}, u32[]{:S(2)}) copy-start(f32[1024]{0:T(1024)S(1)} %get-tuple-element.10) | copy-start | bytes 12292
  305.4 10.2 %slice-start.4 = ((s8[5242880]{0:T(1024)(128)(4,1)}), s8[4194304]{0:T(1024)(128)(4,1)S(1)}, s32[]{:S(2)}) async-start(s8[5242880]{0:T(1024)(128)(4,1)} %bitcast.47), calls=%async_computation.8 | async-start | bytes 8388608
  308.5 7.2 %slice-start.5 = ((s8[5242880]{0:T(1024)(128)(4,1)}), s8[1048576]{0:T(1024)(128)(4,1)S(1)}, s32[]{:S(2)}) async-start(s8[5242880]{0:T(1024)(128)(4,1)} %bitcast.47), calls=%async_computation.9 | async-start | bytes 2097152
Sparse Core Ops, SparseCore 0:
  21.8 76.3 all-gather.3
  121.8 172.6 all-reduce.2
where the time goes:
time: 403 us; the launch traced here: 402 us
  waiting for transfers between devices  197 us (49%)
  blocking collectives  128 us (32%)
  matrix products  30.3 us (8%)
  between operations  16.7 us (4%)
  other arithmetic  14.6 us (4%)
  local copies, waits for them, and re-layouts  12 us (3%)
  starting transfers between devices  4.05 us (1%)
    psum x1, waiting for transfers between devices, shards(): summed = lax.psum(partial_sum, 'latent')  168 us
    psum x1, blocking collectives, shards(): grad_dec, loss_sum = lax.psum((bias_term, loss_term), ('expert', 'latent'))  75.9 us
    all_gather x1, blocking collectives, shards(): lax.all_gather(got_lists[None], 'latent', axis=0, tiled=True)  40.8 us
    all_gather x1, waiting for transfers between devices, shards(): lax.all_gather(got_rows[None], 'latent', axis=0, tiled=True)  24 us
    all_to_all x1, blocking collectives, shards(): lax.all_to_all(send_rows, 'expert', split_axis=0, concat_axis=0, tiled=True)  11.2 us
    dot_general x1, matrix products, shards(): jnp.dot(shifted, weights_here, preferred_element_type=jnp.float32)  8.73 us
  transfers between devices with their start and end apart: 3, of which 3 were waited for; matrix products, arithmetic and copies ran while one was open for 2% of the time, Pallas kernels for 0%

commit v1 on v0

--- a/solution.py
+++ b/solution.py
@@ -51,7 +51,9 @@
     partial_sum = lax.dot_general(
         active_bf, weights_here, along_width, preferred_element_type=jnp.float32
     )
-    summed = lax.psum(partial_sum, "latent")
+    summed = partial_sum
+    for hop in (1, 2, 4, 8, 16):
+        summed = summed + lax.ppermute(summed, "latent", [(dev, dev ^ hop) for dev in range(32)])
     error_all = (summed + dec_bias - rows_f32) * valid[:, None]
     error_bf = error_all.astype(jnp.bfloat16)
     error_share = lax.dynamic_slice_in_dim(error_all, first_row, share, 0)

time: 403 us -> 1040 us (2.58)
  waiting for transfers between devices: 197 us -> 819 us
    ppermute x0 -> x5, waiting for transfers between devices: none -> 791 us  [shards(): lax.ppermute(summed, 'latent', [(dev, dev ^ hop) for dev in range(32)])]
    psum x1 -> x0, waiting for transfers between devices: 168 us -> none  [shards(): summed = lax.psum(partial_sum, 'latent')]
  transfers between devices with their start and end apart: 3 -> 7, of which waited for: 3 -> 7; matrix products, arithmetic and copies ran while one was open for 2% -> 1% of each run, Pallas kernels for 0% -> 0%
where the time goes in v1:
time: 1040 us
  waiting for transfers between devices  819 us (79%)
  blocking collectives  127 us (12%)
  matrix products  31.8 us (3%)
  other arithmetic  23.3 us (2%)
  between operations  16.8 us (2%)
    ppermute x5, waiting for transfers between devices, shards(): lax.ppermute(summed, 'latent', [(dev, dev ^ hop) for dev in range(32)])  791 us
    psum x1, blocking collectives, shards(): grad_dec, loss_sum = lax.psum((bias_term, loss_term), ('expert', 'latent'))  75.2 us
    all_gather x1, blocking collectives, shards(): lax.all_gather(got_lists[None], 'latent', axis=0, tiled=True)  40.8 us
    all_gather x1, waiting for transfers between devices, shards(): lax.all_gather(got_rows[None], 'latent', axis=0, tiled=True)  24 us
  transfers between devices with their start and end apart: 7, of which 7 were waited for; matrix products, arithmetic and copies ran while one was open for 1% of the time, Pallas kernels for 0%

profile of v1, /device:TPU:1, one launch (start us, length us, event | category | flops | bytes accessed | tf_op | source)
XLA Modules:
  0.0 1036.1 jit_solution(13250028458520086978)
XLA Ops:
  7.2 0.0 copy-start.6
  7.2 0.0 all-gather.4.cloned.1.call-start
  7.2 0.7 fusion.24
  8.0 0.8 select_reduce_fusion
  8.8 0.7 fusion.25
  9.5 0.9 scatter_custom_fusion
  10.4 11.2 %all_to_all.10 = bf16[8,2,2560]{2,1,0:T(2,128)(2,1)} all-to-all(bf16[8,2,2560]{2,1,0:T(2,128)(2,1)S(1)} %reshape.33), channel_id=1, replica_groups=mesh['expert'=8,'latent'=32] {'expert'}, dimensions={0} | all-to-all | bytes 163840 | tf_op jit(solution)/shard_map/all_to_all | solution.py:26
  21.6 0.0 all-gather.4.cloned.1.call-update
  21.7 0.8 scatter_custom_fusion.1
  22.4 0.7 reshape.68
  23.1 4.0 all-to-all-start.1
  27.1 4.5 all-to-all-done.1
  31.6 0.5 broadcast.43
  32.2 0.7 reduce.4
  32.8 0.1 reshape.69
  32.9 40.8 %all-gather.1 = s32[256,2,64]{2,1,0:T(2,128)S(1)} all-gather(s32[8,2,64]{2,1,0:T(2,128)S(1)} %reshape.69), channel_id=3, replica_groups=mesh['expert'=8,'latent'=32] {'latent'}, dimensions={0}, use_global_device_ids=true | all-gather | bytes 135168 | tf_op jit(solution)/shard_map/all_gather | solution.py:31
  73.7 0.1 copy.12
  73.8 0.2 compare_reduce_fusion
  74.1 0.1 copy.13
  74.2 24.0 %all-gather.4.cloned.1.call-done = bf16[256,2,2560]{2,1,0:T(2,128)(2,1)} async-done(((bf16[8,2,2560]{2,1,0:T(2,128)(2,1)}), bf16[256,2,2560]{2,1,0:T(2,128)(2,1)}) %all-gather.4.cloned.1.call-update) | async-done | bytes 2621456 | tf_op jit(solution)/shard_map/all_gather | solution.py:30
  98.1 3.5 convert_element_type.56
  101.7 0.0 copy-done.6
  101.7 2.3 subtract_convert_fusion
  104.0 0.0 copy-start.8
  104.0 2.4 convert_element_type.47
  106.4 0.6 broadcast_in_dim.32
  107.0 0.0 copy-start.2
  107.1 0.0 copy-done.8
  107.1 0.0 slice-start.1
  107.1 8.7 fusion.11
  115.8 0.0 copy-done.2
  115.8 2.9 fusion.4
  118.8 0.6 collective-permute-start
  119.4 110.1 %collective-permute-done = f32[512,2560]{1,0:T(8,128)S(1)} collective-permute-done((f32[512,2560]{1,0:T(8,128)S(1)}, f32[512,2560]{1,0:T(8,128)S(1)}, u32[]{:S(2)}, u32[]{:S(2)}) %collective-permute-start) | collective-permute-done | bytes 5242912 | tf_op jit(solution)/shard_map/ppermute | solution.py:56
  229.5 0.9 add.67
  230.4 1.0 collective-permute-start.1
  231.5 226.4 %collective-permute-done.1 = f32[512,2560]{1,0:T(8,128)S(1)} collective-permute-done((f32[512,2560]{1,0:T(8,128)S(1)}, f32[512,2560]{1,0:T(8,128)S(1)}, u32[]{:S(2)}, u32[]{:S(2)}) %collective-permute-start.1) | collective-permute-done | bytes 5242912 | tf_op jit(solution)/shard_map/ppermute | solution.py:56
  457.9 0.9 add.68
  458.8 2.8 collective-permute-start.2
  461.6 228.1 %collective-permute-done.2 = f32[512,2560]{1,0:T(8,128)S(1)} collective-permute-done((f32[512,2560]{1,0:T(8,128)S(1)}, f32[512,2560]{1,0:T(8,128)S(1)}, u32[]{:S(2)}, u32[]{:S(2)}) %collective-permute-start.2) | collective-permute-done | bytes 5242912 | tf_op jit(solution)/shard_map/ppermute | solution.py:56
  689.7 0.9 add.69
  690.7 0.1 collective-permute-start.3
  690.8 114.1 %collective-permute-done.3 = f32[512,2560]{1,0:T(8,128)S(1)} collective-permute-done((f32[512,2560]{1,0:T(8,128)S(1)}, f32[512,2560]{1,0:T(8,128)S(1)}, u32[]{:S(2)}, u32[]{:S(2)}) %collective-permute-start.3) | collective-permute-done | bytes 5242912 | tf_op jit(solution)/shard_map/ppermute | solution.py:56
  804.9 3.3 add.70
  808.1 0.0 collective-permute-start.4
  808.1 0.1 convert_reduce_fusion
  808.3 0.0 copy-done.1
  808.3 2.9 reshape.36
  811.2 112.0 %collective-permute-done.4 = f32[512,2560]{1,0:T(8,128)} collective-permute-done((f32[512,2560]{1,0:T(8,128)}, f32[512,2560]{1,0:T(8,128)}, u32[]{:S(2)}, u32[]{:S(2)}) %collective-permute-start.4) | collective-permute-done | bytes 5242912 | tf_op jit(solution)/shard_map/ppermute | solution.py:56
  923.2 7.5 subtract_multiply_fusion
  930.6 0.0 copy-done.3
  930.6 0.0 copy-done.9
  930.7 0.0 copy-start
  930.7 5.8 fusion.26
  936.5 0.0 copy-start.7
  936.5 0.0 copy-done
  936.5 0.0 copy-start.5
  936.5 0.0 slice-start.2
  936.6 5.6 fusion.9
  942.2 7.3 fusion.8
  949.4 0.6 multiply_reduce_fusion
  950.1 0.0 copy-done.7
  950.1 1.5 fusion.16
  952.3 75.2 %all-reduce = (f32[2560]{0:T(1024)}, f32[]{:T(128)}) all-reduce(f32[2560]{0:T(1024)S(1)} %sub.28, f32[]{:T(128)S(6)} %mul_shard_map.3), channel_id=1, replica_groups=mesh['expert'=8,'latent'=32] {'expert','latent'}, use_global_device_ids=true, to_apply=%region_7.8 | all-reduce | flops 2561 | bytes 20488 | tf_op jit(solution)/shard_map/psum | solution.py:76
  (21 shorter events, 0.1 us)
Async XLA Ops:
  7.2 94.5 %copy-start.6 = (f32[2560]{0:T(1024)S(1)}, f32[2560]{0:T(1024)}, u32[]{:S(2)}) copy-start(f32[2560]{0:T(1024)} %param.11) | copy-start | bytes 30724
  7.2 91.0 %all-gather.4.cloned.1.call-start = ((), (), s32[]{:S(2)}) async-start(), calls=%async_computation.2 | async-start | bytes 2703360 | tf_op jit(solution)/shard_map/all_gather | solution.py:30
  23.1 8.5 all-to-all-start.1
  104.0 3.1 copy-start.8
  106.4 9.4 slice-start
  107.0 8.8 copy-start.2
  107.1 8.8 slice-start.1
  115.8 3.0 copy-start.4
  118.8 110.7 %collective-permute-start = (f32[512,2560]{1,0:T(8,128)S(1)}, f32[512,2560]{1,0:T(8,128)S(1)}, u32[]{:S(2)}, u32[]{:S(2)}) collective-permute-start(f32[512,2560]{1,0:T(8,128)S(1)} %fusion.4), channel_id=1, source_target_pairs={{0,1},{1,0},{2,3},{3,2},{4,5},{5,4},{6,7},{7,6},{8,9},{9,8},{10,11... | collective-permute-start | bytes 15728648 | tf_op jit(solution)/shard_map/ppermute | solution.py:56
  230.4 227.4 %collective-permute-start.1 = (f32[512,2560]{1,0:T(8,128)S(1)}, f32[512,2560]{1,0:T(8,128)S(1)}, u32[]{:S(2)}, u32[]{:S(2)}) collective-permute-start(f32[512,2560]{1,0:T(8,128)S(1)} %add.67), channel_id=1, source_target_pairs={{0,2},{1,3},{2,0},{3,1},{4,6},{5,7},{6,4},{7,5},{8,10},{9,11},{10,... | collective-permute-start | bytes 15728648 | tf_op jit(solution)/shard_map/ppermute | solution.py:56
  458.8 230.9 %collective-permute-start.2 = (f32[512,2560]{1,0:T(8,128)S(1)}, f32[512,2560]{1,0:T(8,128)S(1)}, u32[]{:S(2)}, u32[]{:S(2)}) collective-permute-start(f32[512,2560]{1,0:T(8,128)S(1)} %add.68), channel_id=1, source_target_pairs={{0,4},{1,5},{2,6},{3,7},{4,0},{5,1},{6,2},{7,3},{8,12},{9,13},{10,... | collective-permute-start | bytes 15728648 | tf_op jit(solution)/shard_map/ppermute | solution.py:56
  690.7 117.6 %copy-start.1 = (bf16[256,2,2560]{2,1,0:T(2,128)(2,1)S(1)}, bf16[256,2,2560]{2,1,0:T(2,128)(2,1)}, u32[]{:S(2)}) copy-start(bf16[256,2,2560]{2,1,0:T(2,128)(2,1)} %all-gather.4.cloned.1.call-done) | copy-start | bytes 7864324
  690.7 114.2 %collective-permute-start.3 = (f32[512,2560]{1,0:T(8,128)S(1)}, f32[512,2560]{1,0:T(8,128)S(1)}, u32[]{:S(2)}, u32[]{:S(2)}) collective-permute-start(f32[512,2560]{1,0:T(8,128)S(1)} %add.69), channel_id=1, source_target_pairs={{0,8},{1,9},{2,10},{3,11},{4,12},{5,13},{6,14},{7,15},{8,0},{9,1},... | collective-permute-start | bytes 15728648 | tf_op jit(solution)/shard_map/ppermute | solution.py:56
  808.1 115.0 %collective-permute-start.4 = (f32[512,2560]{1,0:T(8,128)}, f32[512,2560]{1,0:T(8,128)}, u32[]{:S(2)}, u32[]{:S(2)}) collective-permute-start(f32[512,2560]{1,0:T(8,128)} %add.70), channel_id=1, source_target_pairs={{0,16},{1,17},{2,18},{3,19},{4,20},{5,21},{6,22},{7,23},{8,24},{9,... | collective-permute-start | bytes 15728648 | tf_op jit(solution)/shard_map/ppermute | solution.py:56
  811.2 119.4 %copy-start.3 = (f32[512,8,128]{2,1,0:T(8,128)S(1)}, f32[512,8,128]{2,1,0:T(8,128)}, u32[]{:S(2)}) copy-start(f32[512,8,128]{2,1,0:T(8,128)} %copy-done.2) | copy-start | bytes 6291460
  811.2 119.4 %copy-start.9 = (f32[512,1024]{1,0:T(8,128)S(1)}, f32[512,1024]{1,0:T(8,128)}, u32[]{:S(2)}) copy-start(f32[512,1024]{1,0:T(8,128)} %get-tuple-element.9) | copy-start | bytes 6291460
  930.7 5.9 copy-start
  936.5 13.6 %copy-start.7 = (f32[1024]{0:T(1024)}, f32[1024]{0:T(1024)S(1)}, u32[]{:S(2)}) copy-start(f32[1024]{0:T(1024)S(1)} %get-tuple-element.10) | copy-start | bytes 12292
  936.5 5.6 copy-start.5
  936.5 13.5 %slice-start.2 = ((s8[5242880]{0:T(1024)(128)(4,1)}), s8[4194304]{0:T(1024)(128)(4,1)S(1)}, s32[]{:S(2)}) async-start(s8[5242880]{0:T(1024)(128)(4,1)} %bitcast.45), calls=%async_computation.5 | async-start | bytes 8388608
  942.2 7.9 slice-start.3
Sparse Core Ops, SparseCore 0:
  21.8 76.3 all-gather.3
